TPU v7x, 32 devices: a whole 2x2x4 slice. The times are simulated.
32 devices in a mesh: row: 4 (over x, core), col: 8 (over z, y).
Axes of the slice: x: 2, y: 2, z: 4, core: 2. Of those that a mesh axis runs over, the one named last changes fastest.
Arguments:
- fiber_rows: bfloat16 [16384, 1024], P(('row', 'col')), may hold values from -6 to 6
- fiber_i: int32 [16384], P(('row', 'col')), may hold values from 0 to 4095
- fiber_j: int32 [16384], P(('row', 'col')), may hold values from 0 to 65535, as said below
- fiber_count: int32 [32], P(('row', 'col')), may hold values from 256 to 512, as said below
- factor_two: bfloat16 [65536, 32], P('col'), may hold values from -1 to 1
Outputs:
- mode_one: bfloat16 [4096, 32768], P(('row', 'col'))
Inputs may be any that keep to these rules, and one draw needn't show every extreme that they name: fiber_j of a slot on the device with index c along col lies in c * 8192 to (c + 1) * 8192 - 1. `fiber_count`: among the live slots of one device at most 32 have fiber_i in the block of 128 indices of one device (block fiber_i // 128, in the order row then col); some device is full and reaches 32 for each block it sends to.
All inputs are finite; a program needn't handle non-finite values.
Results may differ from a plain program's by a relative error of at most 0.001.
Values may be sent and summed in bfloat16 or wider, within the bound.
A program may use at most 128 MiB of HBM per device.

v0:
```python
import jax
import jax.numpy as jnp
from jax import lax
from jax.sharding import PartitionSpec as P

I_DEV = 128


def body(fiber_rows, fiber_i, fiber_j, fiber_count, factor_two):
    devices = lax.axis_size(("row", "col"))
    stored = fiber_rows.shape[0]
    width = fiber_rows.shape[1]
    rank = factor_two.shape[1]
    col_rows = factor_two.shape[0]
    capacity = 2 * stored // devices
    total_slots = devices * capacity
    live = jnp.arange(stored, dtype=jnp.int32) < fiber_count[0]
    target = fiber_i // I_DEV
    member = (
        (target[:, None] == jnp.arange(devices, dtype=jnp.int32)[None, :]) & live[:, None]
    ).astype(jnp.int32)
    before = jnp.cumsum(member, axis=0) - member
    position = jnp.sum(before * member, axis=1)
    slot = jnp.where(live, target * capacity + position, total_slots)
    local_i = fiber_i - target * I_DEV
    rows_buf = jnp.zeros((total_slots, width), jnp.bfloat16).at[slot].set(fiber_rows, mode="drop")
    index_buf = jnp.full((total_slots,), -1, jnp.int32).at[slot].set(local_i, mode="drop")
    local_j = fiber_j - lax.axis_index("col") * col_rows
    own_rows = jnp.take(factor_two, local_j, axis=0)
    extra_buf = jnp.zeros((total_slots, rank), jnp.bfloat16).at[slot].set(own_rows, mode="drop")
    flat = (devices, capacity)
    moved = (
        lax.all_to_all(
            rows_buf.reshape(flat + (width,)),
            ("row", "col"),
            split_axis=0,
            concat_axis=0,
            tiled=True,
        ),
        lax.all_to_all(
            extra_buf.reshape(flat + extra_buf.shape[1:]),
            ("row", "col"),
            split_axis=0,
            concat_axis=0,
            tiled=True,
        ),
        lax.all_to_all(
            index_buf.reshape(flat), ("row", "col"), split_axis=0, concat_axis=0, tiled=True
        ),
    )
    got_rows = moved[0].reshape(total_slots, width)
    got_index = moved[2].reshape(total_slots)
    got_factor = moved[1].reshape(total_slots, rank)
    block = min(512, total_slots)
    nblocks = total_slots // block
    owned = jnp.arange(I_DEV, dtype=jnp.int32)

    def accumulate(total, pieces):
        rows, factors, indices = pieces
        select = (indices[:, None] == owned[None, :]).astype(jnp.bfloat16)
        expanded = (select[:, :, None] * factors[:, None, :]).reshape(block, I_DEV * rank)
        total = total + lax.dot_general(
            expanded, rows, (((0,), (0,)), ((), ())), preferred_element_type=jnp.float32
        )
        return (total, None)

    start = jnp.zeros((I_DEV * rank, width), jnp.float32)
    total, _ = lax.scan(
        accumulate,
        start,
        (
            got_rows.reshape(nblocks, block, width),
            got_factor.reshape(nblocks, block, rank),
            got_index.reshape(nblocks, block),
        ),
    )
    return total.reshape(I_DEV, rank * width).astype(jnp.bfloat16)


def solution(mesh):
    in_specs = (
        P(("row", "col"), None),
        P(("row", "col")),
        P(("row", "col")),
        P(("row", "col")),
        P("col", None),
    )
    out_specs = P(("row", "col"), None)
    return jax.shard_map(body, mesh=mesh, in_specs=in_specs, out_specs=out_specs, check_vma=False)
```

profile of v0, /device:TPU:0, one launch (start us, length us, event | category | flops | bytes accessed | tf_op | source)
XLA Modules:
  0.0 137.1 jit_solution(8713529923863600418)
XLA Ops:
  0.0 0.7 multiply_subtract_fusion
  1.4 1.2 reduce-window.6
  2.5 0.2 slice_reduce_fusion
  2.8 0.1 fusion.14
  2.9 2.4 %scatter_custom_fusion = s32[1024]{0:T(1024)S(1)} fusion(s32[512]{0:T(512)S(1)} %compare_select_fusion.1, s32[512]{0:T(512)S(1)} %get-tuple-element.85, s32[]{:T(128)} %constant.59.clone.1), kind=kCustom, calls=%fused_computation.44 | custom fusion | bytes 4100 | tf_op jit(solution)/shard_map/scatter | solution.py:27
  5.4 0.7 all_to_all.12
  6.1 7.3 %all-to-all-start = ((s32[32,1,32]{2,1,0:T(1,128)}), s32[32,1,32]{2,1,0:T(1,128)S(1)}, u32[]{:S(2)}, u32[]{:S(2)}) async-start(s32[32,1,32]{2,1,0:T(1,128)} %all_to_all.12), calls=%async_computation | async-start | bytes 32768 | tf_op jit(solution)/shard_map/all_to_all | solution.py:47
  13.4 0.7 compare_and_fusion
  14.1 1.9 %copy.17 = bf16[8192,32]{1,0:T(8,128)(2,1)S(1)} copy(bf16[8192,32]{0,1:T(8,128)(2,1)} %param.11) | data formatting | bytes 1048576 | tf_op args[4]
  16.1 3.2 %scatter_custom_fusion.1 = bf16[1024,32]{1,0:T(8,128)(2,1)S(1)} fusion(s32[512]{0:T(512)S(1)} %compare_select_fusion.1, bf16[]{:T(256)} %constant.40.clone.1, pred[512]{0:T(512)(128)(4,1)S(1)} %get-tuple-element.83, bf16[]{:T(256)} %constant.66.clone.1, bf16[8192,32]{1,0:T(8,128)(2,1)S(1)} %copy.17, s32[1024]{0:T(1024)S(1)} %pad_clamp_fusion), kind=kCustom, calls=%fused_computation.16 | custom fusion | flops 16384 | bytes 2167300 | tf_op jit(solution)/shard_map/scatter | solution.py:30
  19.2 0.2 copy.18
  19.4 0.8 reshape.154
  20.3 0.2 all-to-all-done
  20.5 5.6 %all-to-all-start.1 = ((bf16[32,2,512]{2,1,0:T(2,128)(2,1)}), bf16[32,2,512]{2,1,0:T(2,128)(2,1)S(1)}, u32[]{:S(2)}, u32[]{:S(2)}) async-start(bf16[32,2,512]{2,1,0:T(2,128)(2,1)} %reshape.154), calls=%async_computation.1 | async-start | bytes 131072 | tf_op jit(solution)/shard_map/all_to_all | solution.py:40
  26.1 4.8 %scatter_custom_fusion.2 = bf16[1024,1024]{1,0:T(8,128)(2,1)} fusion(s32[512]{0:T(512)S(1)} %compare_select_fusion.1, bf16[512,1024]{1,0:T(8,128)(2,1)} %param.7, bf16[]{:T(256)} %constant.40.clone.1), kind=kCustom, calls=%fused_computation.14 | custom fusion | bytes 2097664 | tf_op jit(solution)/shard_map/scatter | solution.py:26
  30.9 2.5 %all-to-all-done.1 = bf16[32,2,512]{2,1,0:T(2,128)(2,1)S(1)} async-done(((bf16[32,2,512]{2,1,0:T(2,128)(2,1)}), bf16[32,2,512]{2,1,0:T(2,128)(2,1)S(1)}, u32[]{:S(2)}, u32[]{:S(2)}) %all-to-all-start.1) | async-done | bytes 65568 | tf_op jit(solution)/shard_map/all_to_all | solution.py:40
  33.4 3.5 %all-to-all-start.2 = ((bf16[32,32,1024]{2,1,0:T(8,128)(2,1)}), bf16[32,32,1024]{2,1,0:T(8,128)(2,1)S(1)}, u32[]{:S(2)}, u32[]{:S(2)}) async-start(bf16[32,32,1024]{2,1,0:T(8,128)(2,1)} %bitcast.51), calls=%async_computation.2 | async-start | bytes 4194304 | tf_op jit(solution)/shard_map/all_to_all | solution.py:33
  36.9 0.6 broadcast.86
  37.5 0.7 reduce.5
  38.3 0.1 reshape_reshape.9
  38.3 0.2 reshape.155
  38.5 0.1 copy.19
  38.6 0.2 reshape_reshape.10
  38.9 47.9 %all-to-all-done.2 = bf16[32,32,1024]{2,1,0:T(8,128)(2,1)S(1)} async-done(((bf16[32,32,1024]{2,1,0:T(8,128)(2,1)}), bf16[32,32,1024]{2,1,0:T(8,128)(2,1)S(1)}, u32[]{:S(2)}, u32[]{:S(2)}) %all-to-all-start.2) | async-done | bytes 2097184 | tf_op jit(solution)/shard_map/all_to_all | solution.py:33
  86.8 27.7 %while.11 = (s32[]{:T(128)}, f32[4096,1024]{1,0:T(8,128)}, s32[2,512]{1,0:T(2,128)S(1)}, bf16[2,512,32]{1,2,0:T(8,128)(2,1)S(1)}, bf16[2,512,1024]{2,1,0:T(8,128)(2,1)S(1)}, /*index=5*/s32[]{:T(128)}, s32[]{:T(128)}) while((s32[]{:T(128)}, f32[4096,1024]{1,0:T(8,128)}, s32[2,512]{1,0:T(2,128)S(1)}, ...), condition=%wide.region_7.8_spmd.clone, body=%wide.region_6.7_spmd.clone.sunk | while | flops 4305584128 | bytes 43358304 | solution.py:68
  86.9 2.3 %broadcast_multiply_fusion.2 = bf16[512,128,32]{0,2,1:T(8,128)(2,1)} fusion(bf16[512,32]{0,1:T(8,128)(2,1)S(1)} %dynamic-slice_bitcast_fusion.2, bf16[512,128]{0,1:T(8,128)(2,1)S(1)} %fusion.30), kind=kLoop, calls=%fused_computation.6.clone.1 | loop fusion | flops 2097152 | bytes 4358144 | tf_op jit(solution)/shard_map/while/body/eval_jaxpr/mul | solution.py:61
  89.2 10.3 %select_add_fusion.2 = f32[4096,1024]{1,0:T(8,128)} fusion(f32[4096,1024]{1,0:T(8,128)} %get-tuple-element.126, pred[]{:T(512)S(6)} %compare.5, bf16[512,4096]{0,1:T(8,128)(2,1)} %bitcast.49, bf16[2,512,1024]{2,1,0:T(8,128)(2,1)S(1)} %get-tuple-element.136, s32[]{:T(128)} %get-tuple-element.125), kind=kOutput, calls=%fused_computation.5.clone.1 | convolution fusion | flops 4303355904 | bytes 38797316 | tf_op jit(solution)/shard_map/while/body/eval_jaxpr/dot_general | solution.py:62
  99.5 2.3 %broadcast_multiply_fusion.2 = bf16[512,128,32]{0,2,1:T(8,128)(2,1)} fusion(bf16[512,32]{0,1:T(8,128)(2,1)S(1)} %dynamic-slice_bitcast_fusion.2, bf16[512,128]{0,1:T(8,128)(2,1)S(1)} %fusion.30), kind=kLoop, calls=%fused_computation.6.clone.1 | loop fusion | flops 2097152 | bytes 4358144 | tf_op jit(solution)/shard_map/while/body/eval_jaxpr/mul | solution.py:61
  101.8 12.7 %select_add_fusion.2 = f32[4096,1024]{1,0:T(8,128)} fusion(f32[4096,1024]{1,0:T(8,128)} %get-tuple-element.126, pred[]{:T(512)S(6)} %compare.5, bf16[512,4096]{0,1:T(8,128)(2,1)} %bitcast.49, bf16[2,512,1024]{2,1,0:T(8,128)(2,1)S(1)} %get-tuple-element.136, s32[]{:T(128)} %get-tuple-element.125), kind=kOutput, calls=%fused_computation.5.clone.1 | convolution fusion | flops 4303355904 | bytes 38797316 | tf_op jit(solution)/shard_map/while/body/eval_jaxpr/dot_general | solution.py:62
  114.5 9.1 %convert_element_type.22 = bf16[4096,1024]{1,0:T(8,128)(2,1)} convert(f32[4096,1024]{1,0:T(8,128)} %get-tuple-element.37) | non-fusion elementwise | flops 4194304 | bytes 25165824 | tf_op jit(solution)/shard_map/convert_element_type | solution.py:77
  123.6 13.4 %convert_element_type.23 = bf16[128,32768]{1,0:T(8,128)(2,1)} reshape(bf16[4096,1024]{1,0:T(8,128)(2,1)} %convert_element_type.22) | data formatting | bytes 16777216 | tf_op jit(solution)/shard_map/convert_element_type | solution.py:77
  (15 shorter events, 0.2 us)
Async XLA Ops:
  6.1 14.4 %all-to-all-start = ((s32[32,1,32]{2,1,0:T(1,128)}), s32[32,1,32]{2,1,0:T(1,128)S(1)}, u32[]{:S(2)}, u32[]{:S(2)}) async-start(s32[32,1,32]{2,1,0:T(1,128)} %all_to_all.12), calls=%async_computation | async-start | bytes 32768 | tf_op jit(solution)/shard_map/all_to_all | solution.py:47
  20.5 12.9 %all-to-all-start.1 = ((bf16[32,2,512]{2,1,0:T(2,128)(2,1)}), bf16[32,2,512]{2,1,0:T(2,128)(2,1)S(1)}, u32[]{:S(2)}, u32[]{:S(2)}) async-start(bf16[32,2,512]{2,1,0:T(2,128)(2,1)} %reshape.154), calls=%async_computation.1 | async-start | bytes 131072 | tf_op jit(solution)/shard_map/all_to_all | solution.py:40
  33.4 53.4 %all-to-all-start.2 = ((bf16[32,32,1024]{2,1,0:T(8,128)(2,1)}), bf16[32,32,1024]{2,1,0:T(8,128)(2,1)S(1)}, u32[]{:S(2)}, u32[]{:S(2)}) async-start(bf16[32,32,1024]{2,1,0:T(8,128)(2,1)} %bitcast.51), calls=%async_computation.2 | async-start | bytes 4194304 | tf_op jit(solution)/shard_map/all_to_all | solution.py:33
where the time goes:
time: 138 us; the launch traced here: 137 us
  waiting for transfers between devices  50.6 us (37%)
  local copies, waits for them, and re-layouts  25.8 us (19%)
  matrix products  23 us (17%)
  other arithmetic  20.4 us (15%)
  starting transfers between devices  16.5 us (12%)
    all_to_all x1, waiting for transfers between devices, body(): lax.all_to_all(rows_buf.reshape(flat + (width,)), ('row', 'col'), split_a...  47.9 us
    dot_general x2, matrix products, accumulate(): lax.dot_general(expanded, rows, (((0,), (0,)), ((), ())), preferred_eleme...  23 us
    convert_element_type x1, local copies, waits for them, and re-layouts, body(): return total.reshape(I_DEV, rank * width).astype(jnp.bfloat16)  13.4 us
    convert_element_type x1, other arithmetic, body(): return total.reshape(I_DEV, rank * width).astype(jnp.bfloat16)  9.09 us
    all_to_all x1, starting transfers between devices, body(): lax.all_to_all(index_buf.reshape(flat), ('row', 'col'), split_axis=0, con...  7.33 us
    all_to_all x1, starting transfers between devices, body(): lax.all_to_all(extra_buf.reshape(flat + extra_buf.shape[1:]), ('row', 'co...  5.62 us
    scatter x1, local copies, waits for them, and re-layouts, body(): jnp.zeros((total_slots, width), jnp.bfloat16).at[slot]  4.79 us
    mul x2, other arithmetic, accumulate(): select[:, :, None] * factors[:, None, :]  4.57 us
  transfers between devices with their start and end apart: 3, of which 3 were waited for; matrix products, arithmetic and copies ran while one was open for 10% of the time, Pallas kernels for 0%

commit v1 on v0

v1 whole, which is shorter than its diff:
```python
import functools

import jax
import jax.numpy as jnp
from jax import lax
from jax.experimental import pallas as pl
from jax.experimental.pallas import tpu as pltpu
from jax.sharding import PartitionSpec as P

I_DEV = 128
LANES = 128
KBLOCK = 256
MESH = pl.DeviceIdType.MESH
ORDER = (1, 2, 3, 0)


def contract_lanes(a, b):
    return lax.dot_general(a, b, (((1,), (1,)), ((), ())), preferred_element_type=jnp.float32)


def pack_kernel(
    n, cap, halves, steps, count_ref, i_ref, j_ref, rows_ref, factor_ref, out_ref, meta_ref, slot_ref
):
    stored = rows_ref.shape[0]
    rank, col_rows = factor_ref.shape
    block = out_ref.shape[0]
    step = pl.program_id(0)

    @pl.when(step == 0)
    def _():
        index = i_ref[...]
        shift = I_DEV.bit_length() - 1
        target = jnp.right_shift(index, shift)
        local_i = jnp.bitwise_and(index, I_DEV - 1)
        live = lax.broadcasted_iota(jnp.int32, (1, stored), 1) < count_ref[0]
        target = jnp.where(live, target, -1)
        member = lax.broadcasted_iota(jnp.int32, (n, stored), 0) == target
        earlier = lax.broadcasted_iota(jnp.int32, (stored, stored), 0) < lax.broadcasted_iota(
            jnp.int32, (stored, stored), 1
        )
        before = jnp.dot(
            member.astype(jnp.float32).astype(jnp.bfloat16),
            earlier.astype(jnp.float32).astype(jnp.bfloat16),
            preferred_element_type=jnp.float32,
        )
        position = jnp.sum(jnp.where(member, before, 0.0), axis=0, keepdims=True).astype(jnp.int32)
        slot_ref[...] = jnp.where(live, target * cap + position, -1)

        local_j = j_ref[...] - lax.axis_index("col") * col_rows
        high = jnp.right_shift(local_j, KBLOCK.bit_length() - 1)
        low = jnp.bitwise_and(local_j, KBLOCK - 1)
        chosen = lax.broadcasted_iota(jnp.int32, (KBLOCK, stored), 0) == low
        chosen = chosen.astype(jnp.float32).astype(jnp.bfloat16)
        pieces = col_rows // KBLOCK
        stacked = jnp.concatenate(
            [factor_ref[:, k * KBLOCK : (k + 1) * KBLOCK] for k in range(pieces)], axis=0
        )
        looked = jnp.dot(stacked, chosen, preferred_element_type=jnp.float32)
        own = jnp.zeros((rank, stored), jnp.float32)
        for k in range(pieces):
            own = own + jnp.where(high == k, looked[k * rank : (k + 1) * rank], 0.0)

        hc = cap // halves
        part = LANES // halves
        half = jnp.zeros_like(position)
        for h in range(1, halves):
            half = half + (position >= h * hc).astype(jnp.int32)
        half_slot = jnp.where(live, target * hc + position - half * hc, -1)
        place = jnp.broadcast_to(local_i.astype(jnp.float32), (8, stored))
        filler = jnp.zeros((part - rank - 8, stored), jnp.float32)
        chunks = []
        for h in range(halves):
            chunk = jnp.concatenate([own, place, filler], axis=0)
            chunks.append(jnp.where(half == h, chunk, 0.0))
        table = jnp.concatenate(chunks, axis=0).astype(jnp.bfloat16)
        spread = lax.broadcasted_iota(jnp.int32, (n * hc, stored), 0) == half_slot
        spread = spread.astype(jnp.float32).astype(jnp.bfloat16)
        meta_ref[...] = contract_lanes(spread, table).astype(jnp.bfloat16)

    ids = lax.broadcasted_iota(jnp.int32, (block, stored), 0) + step * block
    move = (ids == slot_ref[...]).astype(jnp.float32).astype(jnp.bfloat16)
    out_ref[...] = jnp.dot(move, rows_ref[...], preferred_element_type=jnp.float32).astype(
        jnp.bfloat16
    )


def flip(z, g, groups):
    out = 0
    bit = 1
    while bit < groups:
        out = out + bit * ((z // bit + g // bit) % 2)
        bit *= 2
    return out


def exchange_kernel(
    nrow, ncol, groups, rows_ref, meta_ref, rrows_ref, rmeta_ref, send_sem, recv_sem, own_sem
):
    n = nrow * ncol
    members = n // groups
    per = ncol // groups
    r = lax.axis_index("row")
    c = lax.axis_index("col")
    me = r * ncol + c
    z, y = c // per, c % per
    seat = r * per + y

    barrier = pltpu.get_barrier_semaphore()

    def greet(k, _):
        other = (me + k) % n
        pl.semaphore_signal(
            barrier, inc=1, device_id=(other // ncol, other % ncol), device_id_type=MESH
        )
        return 0

    lax.fori_loop(1, n, greet, 0)
    own_rows = pltpu.make_async_copy(rows_ref.at[me], rrows_ref.at[0, :, seat], own_sem.at[0])
    own_meta = pltpu.make_async_copy(meta_ref.at[me], rmeta_ref.at[0, seat], own_sem.at[1])
    own_rows.start()
    own_meta.start()
    pl.semaphore_wait(barrier, n - 1)

    def copies(g, k):
        tr = (r + k // per) % nrow
        tc = flip(z, g, groups) * per + (y + k % per) % per
        other = tr * ncol + tc
        t = g * members + k
        return (
            pltpu.make_async_remote_copy(
                src_ref=rows_ref.at[other],
                dst_ref=rrows_ref.at[g, :, seat],
                send_sem=send_sem.at[0, t],
                recv_sem=recv_sem.at[0, t],
                device_id=(tr, tc),
                device_id_type=MESH,
            ),
            pltpu.make_async_remote_copy(
                src_ref=meta_ref.at[other],
                dst_ref=rmeta_ref.at[g, seat],
                send_sem=send_sem.at[1, t],
                recv_sem=recv_sem.at[1, t],
                device_id=(tr, tc),
                device_id_type=MESH,
            ),
        )

    for g in ORDER:
        def send(k, _, g=g):
            for copy in copies(g, k):
                copy.start()
            return 0

        lax.fori_loop(1 if g == 0 else 0, members, send, 0)
    for g in ORDER:
        def finish(k, _, g=g):
            for copy in copies(g, k):
                copy.wait_recv()
                copy.wait_send()
            return 0

        lax.fori_loop(1 if g == 0 else 0, members, finish, 0)
    own_rows.wait()
    own_meta.wait()


def contract_kernel(groups, halves, rows_ref, meta_ref, out_ref, factor_ref, select_ref):
    slots, width = rows_ref.shape
    rank = factor_ref.shape[0]
    kgroup = slots // groups
    part = LANES // halves
    span = kgroup // halves
    per = out_ref.shape[1] // width
    step = pl.program_id(0)

    @pl.when(step == 0)
    def _():
        for g in range(groups):
            turned = meta_ref[g * span : (g + 1) * span, :].astype(jnp.float32).T
            for h in range(halves):
                first = g * kgroup + h * span
                factor_ref[:, first : first + span] = turned[h * part : h * part + rank]
                place = turned[h * part + rank : h * part + rank + 1]
                owned = lax.broadcasted_iota(jnp.int32, (I_DEV, span), 0).astype(jnp.float32)
                select_ref[:, first : first + span] = (
                    (owned == place).astype(jnp.float32).astype(jnp.bfloat16)
                )

    select = select_ref[...]
    left = jnp.concatenate(
        [select * factor_ref[pl.ds(step * per + b, 1), :].astype(jnp.bfloat16) for b in range(per)],
        axis=0,
    )
    total = jnp.dot(left, rows_ref[...], preferred_element_type=jnp.float32)
    for b in range(per):
        out_ref[:, b * width : (b + 1) * width] = total[b * I_DEV : (b + 1) * I_DEV].astype(
            jnp.bfloat16
        )


def body(nrow, ncol, fiber_rows, fiber_i, fiber_j, fiber_count, factor_two):
    n = nrow * ncol
    stored, width = fiber_rows.shape
    col_rows, rank = factor_two.shape
    cap = 2 * stored // n
    slots = n * cap
    halves = 2 if cap % 32 == 0 else 1
    hc = cap // halves
    groups = slots // KBLOCK
    members = n // groups
    steps = 4
    whole = lambda s: (0, 0)
    vmem = 60 * 1024 * 1024
    packed, meta = pl.pallas_call(
        functools.partial(pack_kernel, n, cap, halves, steps),
        out_shape=(
            jax.ShapeDtypeStruct((slots, width), jnp.bfloat16),
            jax.ShapeDtypeStruct((n * hc, LANES), jnp.bfloat16),
        ),
        grid=(steps,),
        in_specs=[
            pl.BlockSpec(memory_space=pltpu.SMEM),
            pl.BlockSpec((1, stored), whole),
            pl.BlockSpec((1, stored), whole),
            pl.BlockSpec((stored, width), whole),
            pl.BlockSpec((rank, col_rows), whole),
        ],
        out_specs=(
            pl.BlockSpec((slots // steps, width), lambda s: (s, 0)),
            pl.BlockSpec((n * hc, LANES), whole),
        ),
        scratch_shapes=[pltpu.VMEM((1, stored), jnp.int32)],
        name="pack",
    )(
        fiber_count,
        fiber_i.reshape(1, stored),
        fiber_j.reshape(1, stored),
        fiber_rows,
        factor_two.T,
    )
    got_rows, got_meta = pl.pallas_call(
        functools.partial(exchange_kernel, nrow, ncol, groups),
        out_shape=(
            jax.ShapeDtypeStruct((groups, halves, members, hc, width), jnp.bfloat16),
            jax.ShapeDtypeStruct((groups, members, hc, LANES), jnp.bfloat16),
        ),
        in_specs=[pl.BlockSpec(memory_space=pl.ANY)] * 2,
        out_specs=(pl.BlockSpec(memory_space=pl.ANY),) * 2,
        scratch_shapes=[
            pltpu.SemaphoreType.DMA((2, n)),
            pltpu.SemaphoreType.DMA((2, n)),
            pltpu.SemaphoreType.DMA((2,)),
        ],
        compiler_params=pltpu.CompilerParams(collective_id=0, has_side_effects=True),
        name="exchange",
    )(packed.reshape(n, halves, hc, width), meta.reshape(n, hc, LANES))
    per = 4
    return pl.pallas_call(
        functools.partial(contract_kernel, groups, halves),
        out_shape=jax.ShapeDtypeStruct((I_DEV, rank * width), jnp.bfloat16),
        grid=(rank // per,),
        in_specs=[
            pl.BlockSpec((slots, width), whole),
            pl.BlockSpec((n * hc, LANES), whole),
        ],
        out_specs=pl.BlockSpec((I_DEV, per * width), lambda s: (0, s)),
        scratch_shapes=[
            pltpu.VMEM((rank, slots), jnp.float32),
            pltpu.VMEM((I_DEV, slots), jnp.bfloat16),
        ],
        name="contract",
    )(got_rows.reshape(slots, width), got_meta.reshape(n * hc, LANES))


def solution(mesh):
    in_specs = (
        P(("row", "col"), None),
        P(("row", "col")),
        P(("row", "col")),
        P(("row", "col")),
        P("col", None),
    )
    out_specs = P(("row", "col"), None)
    step = functools.partial(body, mesh.shape["row"], mesh.shape["col"])
    return jax.shard_map(step, mesh=mesh, in_specs=in_specs, out_specs=out_specs, check_vma=False)
```

time: 138 us -> 74.8 us (0.54)
  the two profiles are of different devices: /device:TPU:0 before, /device:TPU:9 now
where the time goes in v1:
time: 74.8 us; the launch traced here: 74.6 us
  Pallas kernels  74 us (99%)
    pallas_call x1, Pallas kernels, body(): pl.pallas_call(functools.partial(exchange_kernel, nrow, ncol, groups), ou...  55.8 us
    pallas_call x1, Pallas kernels, body(): pl.pallas_call(functools.partial(contract_kernel, groups, halves), out_sh...  12.9 us
    pallas_call x1, Pallas kernels, body(): pl.pallas_call(functools.partial(pack_kernel, n, cap, halves, steps), out...  5.27 us

profile of v1, /device:TPU:9, one launch (start us, length us, event | category | flops | bytes accessed | tf_op | source)
XLA Modules:
  0.0 74.6 jit_solution(13975700070732166428)
XLA Ops:
  0.7 5.3 %pack.1 = (bf16[1024,1024]{1,0:T(8,128)(2,1)}, bf16[512,128]{1,0:T(8,128)(2,1)}) custom-call(s32[1]{0:T(128)S(6)} %copy.6.count_ref, s32[1,512]{1,0:T(1,128)} %bitcast.12, s32[1,512]{1,0:T(1,128)} %bitcast.13, bf16[512,1024]{1,0:T(8,128)(2,1)} %rows_ref.1, bf16[32,8192]{1,0:T(8,128)(2,1)} %bitcast.9), custom_call_target="tpu_custom_call" | custom-call | tf_op jit(solution)/shard_map/pack/pallas_call | solution.py:214
  5.9 55.8 %exchange.1 = (bf16[4,2,8,16,1024]{4,3,2,1,0:T(8,128)(2,1)}, bf16[4,8,16,128]{3,2,1,0:T(8,128)(2,1)}) custom-call(bf16[32,2,16,1024]{3,2,1,0:T(8,128)(2,1)} %bitcast.7, bf16[32,16,128]{2,1,0:T(8,128)(2,1)} %bitcast.10), custom_call_target="tpu_custom_call" | custom-call | tf_op jit(solution)/shard_map/exchange/pallas_call | solution.py:241
  61.8 12.9 %contract.1 = bf16[128,32768]{1,0:T(8,128)(2,1)} custom-call(bf16[1024,1024]{1,0:T(8,128)(2,1)} %bitcast.8, bf16[512,128]{1,0:T(8,128)(2,1)} %bitcast.11), custom_call_target="tpu_custom_call" | custom-call | tf_op jit(solution)/shard_map/contract/pallas_call | solution.py:258

commit v2 on v1

--- a/solution.py
+++ b/solution.py
@@ -12,6 +12,7 @@
 KBLOCK = 256
 MESH = pl.DeviceIdType.MESH
 ORDER = (1, 2, 3, 0)
+ARRIVAL = (0, 1, 2, 3)
 
 
 def contract_lanes(a, b):
@@ -93,8 +94,46 @@
     return out
 
 
+def expand(meta, halves, factor_ref, select_ref):
+    span = meta.shape[0]
+    rank = factor_ref.shape[0]
+    part = LANES // halves
+    turned = meta.astype(jnp.float32).T
+    for h in range(halves):
+        first = h * span
+        factor_ref[:, first : first + span] = turned[h * part : h * part + rank]
+        place = turned[h * part + rank : h * part + rank + 1]
+        owned = lax.broadcasted_iota(jnp.int32, (I_DEV, span), 0).astype(jnp.float32)
+        select_ref[:, first : first + span] = (
+            (owned == place).astype(jnp.float32).astype(jnp.bfloat16)
+        )
+
+
+def spread_factors(select, factor_ref, first, count):
+    return jnp.concatenate(
+        [
+            select * factor_ref[pl.ds(first + b, 1), :].astype(jnp.bfloat16)
+            for b in range(count)
+        ],
+        axis=0,
+    )
+
+
 def exchange_kernel(
-    nrow, ncol, groups, rows_ref, meta_ref, rrows_ref, rmeta_ref, send_sem, recv_sem, own_sem
+    nrow,
+    ncol,
+    groups,
+    halves,
+    rows_ref,
+    meta_ref,
+    rrows_ref,
+    rmeta_ref,
+    total_ref,
+    factor_ref,
+    select_ref,
+    send_sem,
+    recv_sem,
+    own_sem,
 ):
     n = nrow * ncol
     members = n // groups
@@ -152,50 +191,89 @@
             return 0
 
         lax.fori_loop(1 if g == 0 else 0, members, send, 0)
+    rank = factor_ref.shape[0]
+    width = total_ref.shape[1]
+    span = rmeta_ref.shape[1] * rmeta_ref.shape[2]
+    kgroup = span * halves
+    per_step = 8
+
+    for place_in_order, g in enumerate(ARRIVAL):
+        def arrive(k, _, g=g):
+            for copy in copies(g, k):
+                copy.wait_recv()
+            return 0
+
+        lax.fori_loop(1 if g == 0 else 0, members, arrive, 0)
+        if g == 0:
+            own_rows.wait()
+            own_meta.wait()
+        if place_in_order == groups - 1:
+            break
+        expand(rmeta_ref[g].reshape(span, LANES), halves, factor_ref, select_ref)
+
+        def multiply(s, _, g=g, place_in_order=place_in_order):
+            select = select_ref[...]
+            left = spread_factors(select, factor_ref, s * per_step, per_step)
+            product = jnp.dot(
+                left, rrows_ref[g].reshape(kgroup, width), preferred_element_type=jnp.float32
+            )
+            span_m = per_step * I_DEV
+            rows = pl.ds(pl.multiple_of(s * span_m, span_m), span_m)
+            if place_in_order > 0:
+                product = product + total_ref[rows, :]
+            total_ref[rows, :] = product
+            return 0
+
+        lax.fori_loop(0, rank // per_step, multiply, 0)
+
     for g in ORDER:
         def finish(k, _, g=g):
             for copy in copies(g, k):
-                copy.wait_recv()
                 copy.wait_send()
             return 0
 
         lax.fori_loop(1 if g == 0 else 0, members, finish, 0)
-    own_rows.wait()
-    own_meta.wait()
-
-
-def contract_kernel(groups, halves, rows_ref, meta_ref, out_ref, factor_ref, select_ref):
-    slots, width = rows_ref.shape
-    rank = factor_ref.shape[0]
-    kgroup = slots // groups
-    part = LANES // halves
-    span = kgroup // halves
-    per = out_ref.shape[1] // width
-    step = pl.program_id(0)
-
-    @pl.when(step == 0)
-    def _():
-        for g in range(groups):
-            turned = meta_ref[g * span : (g + 1) * span, :].astype(jnp.float32).T
-            for h in range(halves):
-                first = g * kgroup + h * span
-                factor_ref[:, first : first + span] = turned[h * part : h * part + rank]
-                place = turned[h * part + rank : h * part + rank + 1]
-                owned = lax.broadcasted_iota(jnp.int32, (I_DEV, span), 0).astype(jnp.float32)
-                select_ref[:, first : first + span] = (
-                    (owned == place).astype(jnp.float32).astype(jnp.bfloat16)
-                )
-
-    select = select_ref[...]
-    left = jnp.concatenate(
-        [select * factor_ref[pl.ds(step * per + b, 1), :].astype(jnp.bfloat16) for b in range(per)],
-        axis=0,
-    )
-    total = jnp.dot(left, rows_ref[...], preferred_element_type=jnp.float32)
-    for b in range(per):
-        out_ref[:, b * width : (b + 1) * width] = total[b * I_DEV : (b + 1) * I_DEV].astype(
-            jnp.bfloat16
-        )
+
+
+def contract_kernel(
+    halves, rows_ref, meta_ref, total_ref, out_ref, stage_ref, factor_ref, select_ref, sem
+):
+    last = ARRIVAL[-1]
+    rank, kgroup = factor_ref.shape
+    width = total_ref.shape[1]
+    per = stage_ref.shape[2] // width
+    steps = rank // per
+    expand(meta_ref[last].reshape(kgroup // halves, LANES), halves, factor_ref, select_ref)
+
+    def copy_out(s, slot):
+        at = pl.multiple_of(s * per * width, per * width)
+        return pltpu.make_async_copy(
+            stage_ref.at[slot], out_ref.at[:, pl.ds(at, per * width)], sem.at[slot]
+        )
+
+    def multiply(s, _):
+        slot = s % 2
+
+        @pl.when(s >= 2)
+        def _():
+            copy_out(s - 2, slot).wait()
+
+        left = spread_factors(select_ref[...], factor_ref, s * per, per)
+        product = jnp.dot(
+            left, rows_ref[last].reshape(kgroup, width), preferred_element_type=jnp.float32
+        )
+        span_m = per * I_DEV
+        product = product + total_ref[pl.ds(pl.multiple_of(s * span_m, span_m), span_m), :]
+        for b in range(per):
+            stage_ref[slot, :, b * width : (b + 1) * width] = product[
+                b * I_DEV : (b + 1) * I_DEV
+            ].astype(jnp.bfloat16)
+        copy_out(s, slot).start()
+        return 0
+
+    lax.fori_loop(0, steps, multiply, 0)
+    copy_out(steps - 2, steps % 2).wait()
+    copy_out(steps - 1, (steps - 1) % 2).wait()
 
 
 def body(nrow, ncol, fiber_rows, fiber_i, fiber_j, fiber_count, factor_two):
@@ -210,7 +288,6 @@
     members = n // groups
     steps = 4
     whole = lambda s: (0, 0)
-    vmem = 60 * 1024 * 1024
     packed, meta = pl.pallas_call(
         functools.partial(pack_kernel, n, cap, halves, steps),
         out_shape=(
@@ -238,38 +315,43 @@
         fiber_rows,
         factor_two.T,
     )
-    got_rows, got_meta = pl.pallas_call(
-        functools.partial(exchange_kernel, nrow, ncol, groups),
+    in_vmem = pl.BlockSpec(memory_space=pltpu.VMEM)
+    got_rows, got_meta, total = pl.pallas_call(
+        functools.partial(exchange_kernel, nrow, ncol, groups, halves),
         out_shape=(
             jax.ShapeDtypeStruct((groups, halves, members, hc, width), jnp.bfloat16),
             jax.ShapeDtypeStruct((groups, members, hc, LANES), jnp.bfloat16),
+            jax.ShapeDtypeStruct((I_DEV * rank, width), jnp.float32),
         ),
         in_specs=[pl.BlockSpec(memory_space=pl.ANY)] * 2,
-        out_specs=(pl.BlockSpec(memory_space=pl.ANY),) * 2,
+        out_specs=(in_vmem, in_vmem, in_vmem),
         scratch_shapes=[
+            pltpu.VMEM((rank, KBLOCK), jnp.float32),
+            pltpu.VMEM((I_DEV, KBLOCK), jnp.bfloat16),
             pltpu.SemaphoreType.DMA((2, n)),
             pltpu.SemaphoreType.DMA((2, n)),
             pltpu.SemaphoreType.DMA((2,)),
         ],
-        compiler_params=pltpu.CompilerParams(collective_id=0, has_side_effects=True),
+        compiler_params=pltpu.CompilerParams(
+            collective_id=0, has_side_effects=True, vmem_limit_bytes=24 * 1024 * 1024
+        ),
         name="exchange",
     )(packed.reshape(n, halves, hc, width), meta.reshape(n, hc, LANES))
     per = 4
     return pl.pallas_call(
-        functools.partial(contract_kernel, groups, halves),
+        functools.partial(contract_kernel, halves),
         out_shape=jax.ShapeDtypeStruct((I_DEV, rank * width), jnp.bfloat16),
-        grid=(rank // per,),
-        in_specs=[
-            pl.BlockSpec((slots, width), whole),
-            pl.BlockSpec((n * hc, LANES), whole),
+        in_specs=[in_vmem, in_vmem, in_vmem],
+        out_specs=pl.BlockSpec(memory_space=pl.ANY),
+        scratch_shapes=[
+            pltpu.VMEM((2, I_DEV, per * width), jnp.bfloat16),
+            pltpu.VMEM((rank, KBLOCK), jnp.float32),
+            pltpu.VMEM((I_DEV, KBLOCK), jnp.bfloat16),
+            pltpu.SemaphoreType.DMA((2,)),
         ],
-        out_specs=pl.BlockSpec((I_DEV, per * width), lambda s: (0, s)),
-        scratch_shapes=[
-            pltpu.VMEM((rank, slots), jnp.float32),
-            pltpu.VMEM((I_DEV, slots), jnp.bfloat16),
-        ],
+        compiler_params=pltpu.CompilerParams(vmem_limit_bytes=24 * 1024 * 1024),
         name="contract",
-    )(got_rows.reshape(slots, width), got_meta.reshape(n * hc, LANES))
+    )(got_rows, got_meta, total)
 
 
 def solution(mesh):

time: 74.8 us -> 70.4 us (0.941)
  Pallas kernels: 74 us -> 67 us
  local copies, waits for them, and re-layouts: 0 us -> 2.49 us
    pallas_call x2, Pallas kernels: 68.7 us -> 61.7 us  [the longest x1 55.5 us: body(): pl.pallas_call(functools.partial(exchange_kernel, nrow, ncol, groups, hal...]
    unnamed x0 -> x4, local copies, waits for them, and re-layouts: none -> 2.49 us
where the time goes in v2:
time: 70.4 us; the launch traced here: 70.2 us
  Pallas kernels  67 us (95%)
  local copies, waits for them, and re-layouts  2.49 us (4%)
    pallas_call x1, Pallas kernels, body(): pl.pallas_call(functools.partial(exchange_kernel, nrow, ncol, groups, hal...  55.5 us
    pallas_call x1, Pallas kernels, body(): pl.pallas_call(functools.partial(contract_kernel, halves), out_shape=jax....  6.21 us
    pallas_call x1, Pallas kernels, body(): pl.pallas_call(functools.partial(pack_kernel, n, cap, halves, steps), out...  5.27 us
    unnamed x4, local copies, waits for them, and re-layouts  2.49 us

profile of v2, /device:TPU:9, one launch (start us, length us, event | category | flops | bytes accessed | tf_op | source)
XLA Modules:
  0.0 70.2 jit_solution(5725493508992139719)
XLA Ops:
  0.7 5.3 %pack.1 = (bf16[1024,1024]{1,0:T(8,128)(2,1)}, bf16[512,128]{1,0:T(8,128)(2,1)}) custom-call(s32[1]{0:T(128)S(6)} %copy.6.count_ref, s32[1,512]{1,0:T(1,128)} %bitcast.8, s32[1,512]{1,0:T(1,128)} %bitcast.9, bf16[512,1024]{1,0:T(8,128)(2,1)} %rows_ref.1, bf16[32,8192]{1,0:T(8,128)(2,1)} %bitcast.7), custom_call_target="tpu_custom_call" | custom-call | tf_op jit(solution)/shard_map/pack/pallas_call | solution.py:291
  5.9 0.0 copy-start
  5.9 1.6 %copy-done = bf16[1024,1024]{1,0:T(8,128)(2,1)S(1)} copy-done((bf16[1024,1024]{1,0:T(8,128)(2,1)S(1)}, bf16[1024,1024]{1,0:T(8,128)(2,1)}, u32[]{:S(2)}) %copy-start) | copy-done | bytes 2097176
  7.5 0.0 copy-start.1
  7.5 0.9 %copy-done.1 = bf16[512,128]{1,0:T(8,128)(2,1)S(1)} copy-done((bf16[512,128]{1,0:T(8,128)(2,1)S(1)}, bf16[512,128]{1,0:T(8,128)(2,1)}, u32[]{:S(2)}) %copy-start.1) | copy-done | bytes 131096
  8.4 55.5 %exchange.1 = (bf16[4,2,8,16,1024]{4,3,2,1,0:T(8,128)(2,1)S(1)}, bf16[4,8,16,128]{3,2,1,0:T(8,128)(2,1)S(1)}, f32[4096,1024]{1,0:T(8,128)S(1)}) custom-call(bf16[32,2,16,1024]{3,2,1,0:T(8,128)(2,1)S(1)} %bitcast.5, bf16[32,16,128]{2,1,0:T(8,128)(2,1)S(1)} %bitcast.6), custom_call_target="tpu_custom_call" | custom-call | tf_op jit(solution)/shard_map/exchange/pallas_call | solution.py:319
  64.0 6.2 %contract.1 = bf16[128,32768]{1,0:T(8,128)(2,1)} custom-call(bf16[4,2,8,16,1024]{4,3,2,1,0:T(8,128)(2,1)S(1)} %get-tuple-element.12.rows_ref, bf16[4,8,16,128]{3,2,1,0:T(8,128)(2,1)S(1)} %get-tuple-element.13.meta_ref, f32[4096,1024]{1,0:T(8,128)S(1)} %get-tuple-element.14.total_ref), custom_call_target="tpu_custom_call" | custom-call | tf_op jit(solution)/shard_map/contract/pallas_call | solution.py:341
Async XLA Ops:
  5.9 1.6 %copy-start = (bf16[1024,1024]{1,0:T(8,128)(2,1)S(1)}, bf16[1024,1024]{1,0:T(8,128)(2,1)}, u32[]{:S(2)}) copy-start(bf16[1024,1024]{1,0:T(8,128)(2,1)} %get-tuple-element.10) | copy-start | bytes 6291460
  7.5 0.9 %copy-start.1 = (bf16[512,128]{1,0:T(8,128)(2,1)S(1)}, bf16[512,128]{1,0:T(8,128)(2,1)}, u32[]{:S(2)}) copy-start(bf16[512,128]{1,0:T(8,128)(2,1)} %get-tuple-element.11) | copy-start | bytes 393220

commit v3 on v2

--- a/solution.py
+++ b/solution.py
@@ -19,70 +19,72 @@
     return lax.dot_general(a, b, (((1,), (1,)), ((), ())), preferred_element_type=jnp.float32)
 
 
-def pack_kernel(
-    n, cap, halves, steps, count_ref, i_ref, j_ref, rows_ref, factor_ref, out_ref, meta_ref, slot_ref
+def pack(
+    n, cap, halves, count_ref, i_ref, j_ref, rows_ref, factor_ref, out_ref, meta_ref, ready
 ):
     stored = rows_ref.shape[0]
     rank, col_rows = factor_ref.shape
-    block = out_ref.shape[0]
-    step = pl.program_id(0)
-
-    @pl.when(step == 0)
-    def _():
-        index = i_ref[...]
-        shift = I_DEV.bit_length() - 1
-        target = jnp.right_shift(index, shift)
-        local_i = jnp.bitwise_and(index, I_DEV - 1)
-        live = lax.broadcasted_iota(jnp.int32, (1, stored), 1) < count_ref[0]
-        target = jnp.where(live, target, -1)
-        member = lax.broadcasted_iota(jnp.int32, (n, stored), 0) == target
-        earlier = lax.broadcasted_iota(jnp.int32, (stored, stored), 0) < lax.broadcasted_iota(
-            jnp.int32, (stored, stored), 1
-        )
-        before = jnp.dot(
-            member.astype(jnp.float32).astype(jnp.bfloat16),
-            earlier.astype(jnp.float32).astype(jnp.bfloat16),
-            preferred_element_type=jnp.float32,
-        )
-        position = jnp.sum(jnp.where(member, before, 0.0), axis=0, keepdims=True).astype(jnp.int32)
-        slot_ref[...] = jnp.where(live, target * cap + position, -1)
-
-        local_j = j_ref[...] - lax.axis_index("col") * col_rows
-        high = jnp.right_shift(local_j, KBLOCK.bit_length() - 1)
-        low = jnp.bitwise_and(local_j, KBLOCK - 1)
-        chosen = lax.broadcasted_iota(jnp.int32, (KBLOCK, stored), 0) == low
-        chosen = chosen.astype(jnp.float32).astype(jnp.bfloat16)
-        pieces = col_rows // KBLOCK
-        stacked = jnp.concatenate(
-            [factor_ref[:, k * KBLOCK : (k + 1) * KBLOCK] for k in range(pieces)], axis=0
-        )
-        looked = jnp.dot(stacked, chosen, preferred_element_type=jnp.float32)
-        own = jnp.zeros((rank, stored), jnp.float32)
-        for k in range(pieces):
-            own = own + jnp.where(high == k, looked[k * rank : (k + 1) * rank], 0.0)
-
-        hc = cap // halves
-        part = LANES // halves
-        half = jnp.zeros_like(position)
-        for h in range(1, halves):
-            half = half + (position >= h * hc).astype(jnp.int32)
-        half_slot = jnp.where(live, target * hc + position - half * hc, -1)
-        place = jnp.broadcast_to(local_i.astype(jnp.float32), (8, stored))
-        filler = jnp.zeros((part - rank - 8, stored), jnp.float32)
-        chunks = []
-        for h in range(halves):
-            chunk = jnp.concatenate([own, place, filler], axis=0)
-            chunks.append(jnp.where(half == h, chunk, 0.0))
-        table = jnp.concatenate(chunks, axis=0).astype(jnp.bfloat16)
-        spread = lax.broadcasted_iota(jnp.int32, (n * hc, stored), 0) == half_slot
-        spread = spread.astype(jnp.float32).astype(jnp.bfloat16)
-        meta_ref[...] = contract_lanes(spread, table).astype(jnp.bfloat16)
-
-    ids = lax.broadcasted_iota(jnp.int32, (block, stored), 0) + step * block
-    move = (ids == slot_ref[...]).astype(jnp.float32).astype(jnp.bfloat16)
-    out_ref[...] = jnp.dot(move, rows_ref[...], preferred_element_type=jnp.float32).astype(
-        jnp.bfloat16
-    )
+    for copy in ready[:3]:
+        copy.wait()
+    index = i_ref[...]
+    shift = I_DEV.bit_length() - 1
+    target = jnp.right_shift(index, shift)
+    local_i = jnp.bitwise_and(index, I_DEV - 1)
+    live = lax.broadcasted_iota(jnp.int32, (1, stored), 1) < count_ref[0]
+    target = jnp.where(live, target, -1)
+    member = lax.broadcasted_iota(jnp.int32, (n, stored), 0) == target
+    earlier = lax.broadcasted_iota(jnp.int32, (stored, stored), 0) < lax.broadcasted_iota(
+        jnp.int32, (stored, stored), 1
+    )
+    before = jnp.dot(
+        member.astype(jnp.float32).astype(jnp.bfloat16),
+        earlier.astype(jnp.float32).astype(jnp.bfloat16),
+        preferred_element_type=jnp.float32,
+    )
+    position = jnp.sum(jnp.where(member, before, 0.0), axis=0, keepdims=True).astype(jnp.int32)
+    slot = jnp.where(live, target * cap + position, -1)
+
+    local_j = j_ref[...] - lax.axis_index("col") * col_rows
+    high = jnp.right_shift(local_j, KBLOCK.bit_length() - 1)
+    low = jnp.bitwise_and(local_j, KBLOCK - 1)
+    chosen = lax.broadcasted_iota(jnp.int32, (KBLOCK, stored), 0) == low
+    chosen = chosen.astype(jnp.float32).astype(jnp.bfloat16)
+    pieces = col_rows // KBLOCK
+    stacked = jnp.concatenate(
+        [factor_ref[:, k * KBLOCK : (k + 1) * KBLOCK] for k in range(pieces)], axis=0
+    )
+    looked = jnp.dot(stacked, chosen, preferred_element_type=jnp.float32)
+    own = jnp.zeros((rank, stored), jnp.float32)
+    for k in range(pieces):
+        own = own + jnp.where(high == k, looked[k * rank : (k + 1) * rank], 0.0)
+
+    hc = cap // halves
+    part = LANES // halves
+    half = jnp.zeros_like(position)
+    for h in range(1, halves):
+        half = half + (position >= h * hc).astype(jnp.int32)
+    half_slot = jnp.where(live, target * hc + position - half * hc, -1)
+    place = jnp.broadcast_to(local_i.astype(jnp.float32), (8, stored))
+    filler = jnp.zeros((part - rank - 8, stored), jnp.float32)
+    chunks = []
+    for h in range(halves):
+        chunk = jnp.concatenate([own, place, filler], axis=0)
+        chunks.append(jnp.where(half == h, chunk, 0.0))
+    table = jnp.concatenate(chunks, axis=0).astype(jnp.bfloat16)
+    spread = lax.broadcasted_iota(jnp.int32, (n * hc, stored), 0) == half_slot
+    spread = spread.astype(jnp.float32).astype(jnp.bfloat16)
+    meta_ref[...] = contract_lanes(spread, table).astype(jnp.bfloat16).reshape(meta_ref.shape)
+
+    ready[3].wait()
+    fiber_rows = rows_ref[...]
+    targets = KBLOCK // cap
+    for step in range(n // targets):
+        ids = lax.broadcasted_iota(jnp.int32, (KBLOCK, stored), 0) + step * KBLOCK
+        move = (ids == slot).astype(jnp.float32).astype(jnp.bfloat16)
+        moved = jnp.dot(move, fiber_rows, preferred_element_type=jnp.float32).astype(jnp.bfloat16)
+        out_ref[step * targets : (step + 1) * targets] = moved.reshape(
+            (targets,) + out_ref.shape[1:]
+        )
 
 
 def flip(z, g, groups):
@@ -124,16 +126,26 @@
     ncol,
     groups,
     halves,
-    rows_ref,
-    meta_ref,
+    count_ref,
+    i_hbm,
+    j_hbm,
+    fiber_hbm,
+    factor_hbm,
     rrows_ref,
     rmeta_ref,
     total_ref,
+    i_ref,
+    j_ref,
+    fiber_ref,
+    own_factor_ref,
+    rows_ref,
+    meta_ref,
     factor_ref,
     select_ref,
     send_sem,
     recv_sem,
     own_sem,
+    in_sem,
 ):
     n = nrow * ncol
     members = n // groups
@@ -153,12 +165,31 @@
         )
         return 0
 
+    ready = (
+        pltpu.make_async_copy(i_hbm, i_ref, in_sem.at[0]),
+        pltpu.make_async_copy(j_hbm, j_ref, in_sem.at[1]),
+        pltpu.make_async_copy(factor_hbm, own_factor_ref, in_sem.at[2]),
+        pltpu.make_async_copy(fiber_hbm, fiber_ref, in_sem.at[3]),
+    )
+    for copy in ready:
+        copy.start()
     lax.fori_loop(1, n, greet, 0)
+    pack(
+        n,
+        halves * rows_ref.shape[2],
+        halves,
+        count_ref,
+        i_ref,
+        j_ref,
+        fiber_ref,
+        own_factor_ref,
+        rows_ref,
+        meta_ref,
+        ready,
+    )
+    pl.semaphore_wait(barrier, n - 1)
     own_rows = pltpu.make_async_copy(rows_ref.at[me], rrows_ref.at[0, :, seat], own_sem.at[0])
     own_meta = pltpu.make_async_copy(meta_ref.at[me], rmeta_ref.at[0, seat], own_sem.at[1])
-    own_rows.start()
-    own_meta.start()
-    pl.semaphore_wait(barrier, n - 1)
 
     def copies(g, k):
         tr = (r + k // per) % nrow
@@ -191,6 +222,8 @@
             return 0
 
         lax.fori_loop(1 if g == 0 else 0, members, send, 0)
+    own_rows.start()
+    own_meta.start()
     rank = factor_ref.shape[0]
     width = total_ref.shape[1]
     span = rmeta_ref.shape[1] * rmeta_ref.shape[2]
@@ -286,35 +319,6 @@
     hc = cap // halves
     groups = slots // KBLOCK
     members = n // groups
-    steps = 4
-    whole = lambda s: (0, 0)
-    packed, meta = pl.pallas_call(
-        functools.partial(pack_kernel, n, cap, halves, steps),
-        out_shape=(
-            jax.ShapeDtypeStruct((slots, width), jnp.bfloat16),
-            jax.ShapeDtypeStruct((n * hc, LANES), jnp.bfloat16),
-        ),
-        grid=(steps,),
-        in_specs=[
-            pl.BlockSpec(memory_space=pltpu.SMEM),
-            pl.BlockSpec((1, stored), whole),
-            pl.BlockSpec((1, stored), whole),
-            pl.BlockSpec((stored, width), whole),
-            pl.BlockSpec((rank, col_rows), whole),
-        ],
-        out_specs=(
-            pl.BlockSpec((slots // steps, width), lambda s: (s, 0)),
-            pl.BlockSpec((n * hc, LANES), whole),
-        ),
-        scratch_shapes=[pltpu.VMEM((1, stored), jnp.int32)],
-        name="pack",
-    )(
-        fiber_count,
-        fiber_i.reshape(1, stored),
-        fiber_j.reshape(1, stored),
-        fiber_rows,
-        factor_two.T,
-    )
     in_vmem = pl.BlockSpec(memory_space=pltpu.VMEM)
     got_rows, got_meta, total = pl.pallas_call(
         functools.partial(exchange_kernel, nrow, ncol, groups, halves),
@@ -323,20 +327,38 @@
             jax.ShapeDtypeStruct((groups, members, hc, LANES), jnp.bfloat16),
             jax.ShapeDtypeStruct((I_DEV * rank, width), jnp.float32),
         ),
-        in_specs=[pl.BlockSpec(memory_space=pl.ANY)] * 2,
+        in_specs=[pl.BlockSpec(memory_space=pltpu.SMEM)] + [pl.BlockSpec(memory_space=pltpu.HBM)] * 4,
         out_specs=(in_vmem, in_vmem, in_vmem),
         scratch_shapes=[
+            pltpu.VMEM((1, stored), jnp.int32),
+            pltpu.VMEM((1, stored), jnp.int32),
+            pltpu.VMEM((stored, width), jnp.bfloat16),
+            pltpu.VMEM((rank, col_rows), jnp.bfloat16),
+            pltpu.VMEM((n, halves, hc, width), jnp.bfloat16),
+            pltpu.VMEM((n, hc, LANES), jnp.bfloat16),
             pltpu.VMEM((rank, KBLOCK), jnp.float32),
             pltpu.VMEM((I_DEV, KBLOCK), jnp.bfloat16),
             pltpu.SemaphoreType.DMA((2, n)),
             pltpu.SemaphoreType.DMA((2, n)),
             pltpu.SemaphoreType.DMA((2,)),
+            pltpu.SemaphoreType.DMA((4,)),
         ],
         compiler_params=pltpu.CompilerParams(
-            collective_id=0, has_side_effects=True, vmem_limit_bytes=24 * 1024 * 1024
+            collective_id=0, has_side_effects=True, vmem_limit_bytes=32 * 1024 * 1024
         ),
         name="exchange",
-    )(packed.reshape(n, halves, hc, width), meta.reshape(n, hc, LANES))
+    )(
+        fiber_count,
+        *(
+            pltpu.with_memory_space_constraint(x, pltpu.HBM)
+            for x in (
+                fiber_i.reshape(1, stored),
+                fiber_j.reshape(1, stored),
+                fiber_rows,
+                factor_two.T,
+            )
+        ),
+    )
     per = 4
     return pl.pallas_call(
         functools.partial(contract_kernel, halves),

time: 70.4 us -> 64.1 us (0.911)
  Pallas kernels: 67 us -> 63.3 us
  local copies, waits for them, and re-layouts: 2.49 us -> 0 us
    pallas_call x1 -> x0, Pallas kernels: 5.27 us -> none  [body(): pl.pallas_call(functools.partial(pack_kernel, n, cap, halves, steps), out...]
    unnamed x4 -> x0, local copies, waits for them, and re-layouts: 2.49 us -> none
    pallas_call x1, Pallas kernels: 55.5 us -> 57.1 us  [body(): pl.pallas_call(functools.partial(exchange_kernel, nrow, ncol, groups, hal...]
where the time goes in v3:
time: 64.1 us; the launch traced here: 64 us
  Pallas kernels  63.3 us (99%)
  between operations  0.66 us (1%)
    pallas_call x1, Pallas kernels, body(): pl.pallas_call(functools.partial(exchange_kernel, nrow, ncol, groups, hal...  57.1 us
    pallas_call x1, Pallas kernels, body(): pl.pallas_call(functools.partial(contract_kernel, halves), out_shape=jax....  6.21 us

profile of v3, /device:TPU:9, one launch (start us, length us, event | category | flops | bytes accessed | tf_op | source)
XLA Modules:
  0.0 64.0 jit_solution(5911589655300781879)
XLA Ops:
  0.7 57.1 %exchange.1 = (bf16[4,2,8,16,1024]{4,3,2,1,0:T(8,128)(2,1)S(1)}, bf16[4,8,16,128]{3,2,1,0:T(8,128)(2,1)S(1)}, f32[4096,1024]{1,0:T(8,128)S(1)}) custom-call(s32[1]{0:T(128)S(6)} %copy.6.count_ref, s32[1,512]{1,0:T(1,128)} %bitcast.4, s32[1,512]{1,0:T(1,128)} %bitcast.5, bf16[512,1024]{1,0:T(8,128)(2,1)} %fiber_hbm.1, bf16[32,8192]{1,0:T(8,128)(2,1)} %bitcast.3), custom_call_target="tpu_custom_call" | custom-call | tf_op jit(solution)/shard_map/exchange/pallas_call | solution.py:323
  57.8 6.2 %contract.1 = bf16[128,32768]{1,0:T(8,128)(2,1)} custom-call(bf16[4,2,8,16,1024]{4,3,2,1,0:T(8,128)(2,1)S(1)} %get-tuple-element.8.rows_ref, bf16[4,8,16,128]{3,2,1,0:T(8,128)(2,1)S(1)} %get-tuple-element.9.meta_ref, f32[4096,1024]{1,0:T(8,128)S(1)} %get-tuple-element.10.total_ref), custom_call_target="tpu_custom_call" | custom-call | tf_op jit(solution)/shard_map/contract/pallas_call | solution.py:363

commit v4 on v3

--- a/solution.py
+++ b/solution.py
@@ -24,8 +24,7 @@
 ):
     stored = rows_ref.shape[0]
     rank, col_rows = factor_ref.shape
-    for copy in ready[:3]:
-        copy.wait()
+    ready[0].wait()
     index = i_ref[...]
     shift = I_DEV.bit_length() - 1
     target = jnp.right_shift(index, shift)
@@ -44,6 +43,20 @@
     position = jnp.sum(jnp.where(member, before, 0.0), axis=0, keepdims=True).astype(jnp.int32)
     slot = jnp.where(live, target * cap + position, -1)
 
+    ready[3].wait()
+    fiber_rows = rows_ref[...]
+    targets = KBLOCK // cap
+    for step in range(n // targets):
+        ids = lax.broadcasted_iota(jnp.int32, (KBLOCK, stored), 0) + step * KBLOCK
+        move = (ids == slot).astype(jnp.float32).astype(jnp.bfloat16)
+        moved = jnp.dot(move, fiber_rows, preferred_element_type=jnp.float32).astype(jnp.bfloat16)
+        out_ref[step * targets : (step + 1) * targets] = moved.reshape(
+            (targets,) + out_ref.shape[1:]
+        )
+    yield
+
+    ready[1].wait()
+    ready[2].wait()
     local_j = j_ref[...] - lax.axis_index("col") * col_rows
     high = jnp.right_shift(local_j, KBLOCK.bit_length() - 1)
     low = jnp.bitwise_and(local_j, KBLOCK - 1)
@@ -74,17 +87,6 @@
     spread = lax.broadcasted_iota(jnp.int32, (n * hc, stored), 0) == half_slot
     spread = spread.astype(jnp.float32).astype(jnp.bfloat16)
     meta_ref[...] = contract_lanes(spread, table).astype(jnp.bfloat16).reshape(meta_ref.shape)
-
-    ready[3].wait()
-    fiber_rows = rows_ref[...]
-    targets = KBLOCK // cap
-    for step in range(n // targets):
-        ids = lax.broadcasted_iota(jnp.int32, (KBLOCK, stored), 0) + step * KBLOCK
-        move = (ids == slot).astype(jnp.float32).astype(jnp.bfloat16)
-        moved = jnp.dot(move, fiber_rows, preferred_element_type=jnp.float32).astype(jnp.bfloat16)
-        out_ref[step * targets : (step + 1) * targets] = moved.reshape(
-            (targets,) + out_ref.shape[1:]
-        )
 
 
 def flip(z, g, groups):
@@ -174,7 +176,7 @@
     for copy in ready:
         copy.start()
     lax.fori_loop(1, n, greet, 0)
-    pack(
+    packing = pack(
         n,
         halves * rows_ref.shape[2],
         halves,
@@ -187,6 +189,7 @@
         meta_ref,
         ready,
     )
+    next(packing)
     pl.semaphore_wait(barrier, n - 1)
     own_rows = pltpu.make_async_copy(rows_ref.at[me], rrows_ref.at[0, :, seat], own_sem.at[0])
     own_meta = pltpu.make_async_copy(meta_ref.at[me], rmeta_ref.at[0, seat], own_sem.at[1])
@@ -215,13 +218,19 @@
             ),
         )
 
+    def send_all(g, which):
+        def send(k, _):
+            copies(g, k)[which].start()
+            return 0
+
+        lax.fori_loop(1 if g == 0 else 0, members, send, 0)
+
+    send_all(ORDER[0], 0)
+    next(packing, None)
     for g in ORDER:
-        def send(k, _, g=g):
-            for copy in copies(g, k):
-                copy.start()
-            return 0
-
-        lax.fori_loop(1 if g == 0 else 0, members, send, 0)
+        send_all(g, 1)
+    for g in ORDER[1:]:
+        send_all(g, 0)
     own_rows.start()
     own_meta.start()
     rank = factor_ref.shape[0]

time: 64.1 us -> 64.3 us (level)
  no operation moved by 1% of the time
where the time goes in v4:
time: 64.3 us; the launch traced here: 64.2 us
  Pallas kernels  63.5 us (99%)
  between operations  0.66 us (1%)
    pallas_call x1, Pallas kernels, body(): pl.pallas_call(functools.partial(exchange_kernel, nrow, ncol, groups, hal...  57.3 us
    pallas_call x1, Pallas kernels, body(): pl.pallas_call(functools.partial(contract_kernel, halves), out_shape=jax....  6.21 us

profile of v4, /device:TPU:9, one launch (start us, length us, event | category | flops | bytes accessed | tf_op | source)
XLA Modules:
  0.0 64.2 jit_solution(6343430434315636040)
XLA Ops:
  0.7 57.3 %exchange.1 = (bf16[4,2,8,16,1024]{4,3,2,1,0:T(8,128)(2,1)S(1)}, bf16[4,8,16,128]{3,2,1,0:T(8,128)(2,1)S(1)}, f32[4096,1024]{1,0:T(8,128)S(1)}) custom-call(s32[1]{0:T(128)S(6)} %copy.6.count_ref, s32[1,512]{1,0:T(1,128)} %bitcast.4, s32[1,512]{1,0:T(1,128)} %bitcast.5, bf16[512,1024]{1,0:T(8,128)(2,1)} %fiber_hbm.1, bf16[32,8192]{1,0:T(8,128)(2,1)} %bitcast.3), custom_call_target="tpu_custom_call" | custom-call | tf_op jit(solution)/shard_map/exchange/pallas_call | solution.py:332
  58.0 6.2 %contract.1 = bf16[128,32768]{1,0:T(8,128)(2,1)} custom-call(bf16[4,2,8,16,1024]{4,3,2,1,0:T(8,128)(2,1)S(1)} %get-tuple-element.8.rows_ref, bf16[4,8,16,128]{3,2,1,0:T(8,128)(2,1)S(1)} %get-tuple-element.9.meta_ref, f32[4096,1024]{1,0:T(8,128)S(1)} %get-tuple-element.10.total_ref), custom_call_target="tpu_custom_call" | custom-call | tf_op jit(solution)/shard_map/contract/pallas_call | solution.py:372
